TPU v7x, 32 devices: a whole 2x2x4 slice. The times are simulated.
32 devices in a mesh: rows: 8 (over z, y), cols: 4 (over x, core).
Axes of the slice: x: 2, y: 2, z: 4, core: 2. Of those that a mesh axis runs over, the one named last changes fastest.
Arguments:
- sketches: bfloat16 [2048, 16384], P('rows', 'cols'), may hold values from -6 to 6, as said below
- start_basis: bfloat16 [16384, 256], P('cols'), may hold values from -6 to 6
- shrink_index: int32 [1], replicated, may hold values from 64 to 191
Outputs:
- shrunk: float32 [256, 16384], P('rows', 'cols')
Inputs may be any that keep to these rules, and one draw needn't show every extreme that they name: `sketches`: real entries.
All inputs are finite; a program needn't handle non-finite values.
Results may differ from a plain program's by a relative error of at most 0.0028.
Values may be sent and summed in bfloat16 or wider, within the bound.
A program may use at most 64 MiB of HBM per device.

v0:
```python
import functools

import jax
import jax.numpy as jnp
from jax import lax
from jax.experimental import pallas as pl
from jax.experimental.pallas import tpu as pltpu
from jax.sharding import PartitionSpec as P

ITERS = 3
AXES = ("rows", "cols")
HIGHEST = lax.Precision.HIGHEST


def pieces(values):
    high = lax.reduce_precision(values, 8, 7)
    rest = values - high
    middle = lax.reduce_precision(rest, 8, 7)
    low = rest - middle
    return [part.astype(jnp.bfloat16) for part in (high, middle, low)]


def apply_sketches(strip, images):
    stacked = jnp.concatenate(pieces(images), axis=1)
    products = jnp.dot(strip, stacked, preferred_element_type=jnp.float32)
    high, middle, low = jnp.split(products, 3, axis=1)
    return high + (middle + low)


def path_orders(sizes):
    cols_bits = [("cols", 1 << bit) for bit in range(sizes["cols"].bit_length() - 1)]
    rows_bits = [("rows", 1 << bit) for bit in range(sizes["rows"].bit_length() - 1)]
    first = cols_bits + rows_bits
    second = cols_bits[:1] + rows_bits + cols_bits[1:]
    return [first, second]


def sum_kernel(orders, x_ref, out_ref, partial, arrived, send_sems, recv_sems):
    index = {axis: lax.axis_index(axis) for axis in AXES}
    stages = len(orders[0])
    rows = x_ref.shape[0] // len(orders)

    def side_of(axis, step):
        return lax.rem(index[axis] // step, 2)

    def partner_of(axis, step):
        return {axis: index[axis] + step * (1 - 2 * side_of(axis, step))}

    barrier = pltpu.get_barrier_semaphore()
    for axis, step in orders[0]:
        pl.semaphore_signal(
            barrier, inc=1, device_id=partner_of(axis, step), device_id_type=pl.DeviceIdType.MESH
        )
    pl.semaphore_wait(barrier, stages)

    copies = []

    def send(path, phase, stage, src, dst):
        copy = pltpu.make_async_remote_copy(
            src_ref=src,
            dst_ref=dst,
            send_sem=send_sems.at[path, phase, stage],
            recv_sem=recv_sems.at[path, phase, stage],
            device_id=partner_of(*orders[path][stage]),
            device_id_type=pl.DeviceIdType.MESH,
        )
        copy.start()
        copies.append(copy)
        return copy

    def span(start, size):
        return pl.ds(pl.multiple_of(start, 8), size)

    lows = [path * rows for path in range(len(orders))]
    trail = [[] for _ in orders]
    pending = [None for _ in orders]

    def halve(path, stage):
        half = rows >> (stage + 1)
        side = side_of(*orders[path][stage])
        source = x_ref if stage == 0 else partial
        slot = path * rows + rows - (rows >> stage)
        pending[path] = send(
            path, 0, stage,
            source.at[span(lows[path] + (1 - side) * half, half), :],
            arrived.at[slot : slot + half, :],
        )
        trail[path].append(lows[path])
        lows[path] = lows[path] + side * half

    for path in range(len(orders)):
        halve(path, 0)
    for stage in range(stages):
        half = rows >> (stage + 1)
        for path in range(len(orders)):
            pending[path].wait_recv()
            slot = path * rows + rows - (rows >> stage)
            own = span(lows[path], half)
            source = x_ref if stage == 0 else partial
            target = out_ref if stage == stages - 1 else partial
            target[own, :] = source[own, :] + arrived[slot : slot + half, :]
            if stage + 1 < stages:
                halve(path, stage + 1)
            else:
                own_rows = out_ref.at[own, :]
                pending[path] = send(path, 1, stage, own_rows, own_rows)
    for stage in reversed(range(stages)):
        for path in range(len(orders)):
            pending[path].wait_recv()
            if stage > 0:
                held = out_ref.at[span(trail[path][stage], rows >> stage), :]
                pending[path] = send(path, 1, stage - 1, held, held)
    for copy in copies:
        copy.wait_send()


def all_sum(values):
    sizes = {axis: lax.axis_size(axis) for axis in AXES}
    orders = path_orders(sizes)
    stages = len(orders[0])
    return pl.pallas_call(
        functools.partial(sum_kernel, orders),
        out_shape=jax.ShapeDtypeStruct(values.shape, jnp.float32),
        in_specs=[pl.BlockSpec(memory_space=pltpu.VMEM)],
        out_specs=pl.BlockSpec(memory_space=pltpu.VMEM),
        scratch_shapes=[
            pltpu.VMEM(values.shape, jnp.float32),
            pltpu.VMEM(values.shape, jnp.float32),
            pltpu.SemaphoreType.DMA((len(orders), 2, stages)),
            pltpu.SemaphoreType.DMA((len(orders), 2, stages)),
        ],
        compiler_params=pltpu.CompilerParams(
            collective_id=0, has_side_effects=True, vmem_limit_bytes=48 << 20
        ),
        name="all_sum",
    )(values)


def start_kernel(sizes, x_ref, out_ref, partial, arrived, send_sems, recv_sems):
    index = {axis: lax.axis_index(axis) for axis in AXES}
    bits = {axis: [1 << bit for bit in range(sizes[axis].bit_length() - 1)] for axis in AXES}

    def side_of(axis, step):
        return lax.rem(index[axis] // step, 2)

    def partner_of(axis, step):
        return {axis: index[axis] + step * (1 - 2 * side_of(axis, step))}

    barrier = pltpu.get_barrier_semaphore()
    for axis in AXES:
        for step in bits[axis]:
            pl.semaphore_signal(
                barrier, inc=1, device_id=partner_of(axis, step), device_id_type=pl.DeviceIdType.MESH
            )
    pl.semaphore_wait(barrier, len(bits["rows"]) + len(bits["cols"]))

    copies = []

    def send(axis, step, src, dst):
        number = len(copies)
        copy = pltpu.make_async_remote_copy(
            src_ref=src,
            dst_ref=dst,
            send_sem=send_sems.at[number],
            recv_sem=recv_sems.at[number],
            device_id=partner_of(axis, step),
            device_id_type=pl.DeviceIdType.MESH,
        )
        copy.start()
        copies.append(copy)
        copy.wait_recv()

    def span(start, size):
        return pl.ds(pl.multiple_of(start, 16), size)

    count = x_ref.shape[0]
    low = 0
    lows = []
    source = x_ref
    for step in bits["cols"]:
        half = count // 2
        side = side_of("cols", step)
        slot = x_ref.shape[0] - count
        send(
            "cols", step,
            source.at[span(low + (1 - side) * half, half), :],
            arrived.at[slot : slot + half, :],
        )
        lows.append(low)
        low = low + side * half
        own = span(low, half)
        partial[own, :] = source[own, :] + arrived[slot : slot + half, :]
        source = partial
        count = half
    me = index["rows"]
    out_ref[pl.ds(me, 1), span(low, count), :] = source[span(low, count), :].astype(out_ref.dtype)[None]
    for step in bits["rows"]:
        held = out_ref.at[pl.ds(me // step * step, step), span(low, count), :]
        send("rows", step, held, held)
    for step, before in zip(reversed(bits["cols"]), reversed(lows)):
        held = out_ref.at[:, span(low, count), :]
        send("cols", step, held, held)
        low = before
        count = count * 2
    for copy in copies:
        copy.wait_send()


def start_sum(values):
    sizes = {axis: lax.axis_size(axis) for axis in AXES}
    sends = 2 * (sizes["cols"].bit_length() - 1) + sizes["rows"].bit_length() - 1
    owned, rank = values.shape
    gathered = pl.pallas_call(
        functools.partial(start_kernel, sizes),
        out_shape=jax.ShapeDtypeStruct((sizes["rows"], owned, rank), jnp.bfloat16),
        in_specs=[pl.BlockSpec(memory_space=pltpu.VMEM)],
        out_specs=pl.BlockSpec(memory_space=pltpu.VMEM),
        scratch_shapes=[
            pltpu.VMEM(values.shape, jnp.float32),
            pltpu.VMEM(values.shape, jnp.float32),
            pltpu.SemaphoreType.DMA((sends,)),
            pltpu.SemaphoreType.DMA((sends,)),
        ],
        compiler_params=pltpu.CompilerParams(
            collective_id=1, has_side_effects=True, vmem_limit_bytes=32 << 20
        ),
        name="start_sum",
    )(values)
    return gathered.reshape(sizes["rows"] * owned, rank)


TILE = 128
SUBLANES = 8
PIVOTS = 4


def dot_full(left, right, contract=((1,), (0,))):
    return lax.dot_general(
        left, right, (contract, ((), ())), precision=HIGHEST, preferred_element_type=jnp.float32
    )


def eliminate(block):
    count = TILE // SUBLANES
    row_at = lax.broadcasted_iota(jnp.int32, (SUBLANES, TILE), 0)
    lane_at = lax.broadcasted_iota(jnp.int32, (SUBLANES, TILE), 1)
    left = [block[v * SUBLANES : (v + 1) * SUBLANES, :] for v in range(count)]
    right = [(lane_at == row_at + v * SUBLANES).astype(jnp.float32) for v in range(count)]
    done = []
    pivots = jnp.ones((SUBLANES, TILE), jnp.float32)
    def spread(row):
        return jnp.broadcast_to(row, (SUBLANES, TILE))

    for j in range(0, TILE, PIVOTS):
        first, k = divmod(j, SUBLANES)
        heads = [spread(left[first][:, j + i : j + i + 1]) for i in range(PIVOTS)]
        inverses, across = [], {}
        for i in range(PIVOTS):
            pivot = heads[i][k + i : k + i + 1, :]
            inverses.append(1.0 / pivot)
            pivots = jnp.where(row_at == k + i, spread(pivot), pivots)
            below = jnp.where(row_at > k + i, heads[i], 0.0)
            for n in range(i + 1, PIVOTS):
                across[i, n] = heads[n][k + i : k + i + 1, :] * inverses[i]
                heads[n] = heads[n] - below * across[i, n]
            heads[i] = below
        rows = []
        for side in (left, right):
            current, scaled = side[first], []
            for i in range(PIVOTS):
                scaled.append(current[k + i : k + i + 1, :] * inverses[i])
                current = current - heads[i] * scaled[i]
            side[first] = current
            rows.append(scaled)
        for v in range(first + 1, count):
            scales = [spread(left[v][:, j + i : j + i + 1]) for i in range(PIVOTS)]
            for i in range(PIVOTS):
                for n in range(i + 1, PIVOTS):
                    scales[n] = scales[n] - scales[i] * across[i, n]
                left[v] = left[v] - scales[i] * rows[0][i]
                right[v] = right[v] - scales[i] * rows[1][i]
        if k + PIVOTS == SUBLANES:
            done.append(right[first] / jnp.sqrt(pivots))
    return jnp.concatenate(done, axis=0)


def factor_kernel(gram_ref, inverse_ref, work_ref, lower_ref):
    size = gram_ref.shape[0]
    inverse_ref[...] = jnp.zeros_like(inverse_ref)
    work_ref[...] = gram_ref[:TILE, :TILE]

    @pl.loop(0, size // TILE)
    def _(at):
        own = eliminate(work_ref[...])
        work_ref[...] = own
        for number in range(size // TILE):
            start, stop = number * TILE, (number + 1) * TILE
            here = slice(start, stop)

            @pl.when(at == number)
            def _():
                inverse_ref[here, here] = work_ref[...]
                if start > 0:
                    off = dot_full(lower_ref[:, :start], inverse_ref[:start, :start])
                    inverse_ref[here, :start] = -dot_full(work_ref[...], off)
                if stop < size:
                    after = slice(stop, stop + TILE)
                    lower = dot_full(gram_ref[after, :stop], inverse_ref[:stop, :stop], ((1,), (1,)))
                    lower_ref[:, :stop] = lower
                    work_ref[...] = gram_ref[after, after] - dot_full(lower, lower, ((1,), (1,)))


def inverse_factor(gram_total):
    return pl.pallas_call(
        factor_kernel,
        out_shape=jax.ShapeDtypeStruct(gram_total.shape, jnp.float32),
        in_specs=[pl.BlockSpec(memory_space=pltpu.VMEM)],
        out_specs=pl.BlockSpec(memory_space=pltpu.VMEM),
        scratch_shapes=[
            pltpu.VMEM((TILE, TILE), jnp.float32),
            pltpu.VMEM((TILE, gram_total.shape[0]), jnp.float32),
        ],
        name="factor",
    )(gram_total)


def body(sketches, start_basis, shrink_index):
    strip = lax.all_to_all(sketches, "rows", split_axis=1, concat_axis=0, tiled=True)
    projected_bf = start_sum(jnp.dot(sketches, start_basis, preferred_element_type=jnp.float32))
    for loop_index in range(ITERS):
        if loop_index > 0:
            projected_bf = projected.astype(jnp.bfloat16)
        images = jnp.einsum("lw,lk->wk", strip, projected_bf, preferred_element_type=jnp.float32)
        raw = all_sum(apply_sketches(strip, images))
        gram_total = jnp.dot(projected_bf.astype(jnp.float32).T, raw, precision=HIGHEST)
        gram_total = 0.5 * (gram_total + gram_total.T)
        inverse = inverse_factor(gram_total)
        projected = jnp.dot(raw, inverse.T, precision=HIGHEST)
    energy = jnp.sum(projected * projected, axis=0)
    ordered = jnp.sort(energy)[::-1]
    threshold = lax.dynamic_index_in_dim(ordered, shrink_index[0], 0, keepdims=False)
    factor = jnp.sqrt(jnp.maximum(energy - threshold, 0.25 * threshold))
    scaled = jnp.dot(inverse * factor[:, None], images.T, precision=HIGHEST)
    return lax.all_to_all(scaled, "rows", split_axis=0, concat_axis=1, tiled=True)


def solution(mesh):
    return jax.shard_map(
        body,
        mesh=mesh,
        in_specs=(P("rows", "cols"), P("cols", None), P()),
        out_specs=P("rows", "cols"),
        check_vma=False,
    )
```

profile of v0, /device:TPU:0, one launch (start us, length us, event | category | flops | bytes accessed | tf_op | source)
XLA Modules:
  0.0 313.0 jit_solution(17863644920457570349)
XLA Ops:
  0.0 0.0 copy-start
  0.0 4.3 %copy.12 = bf16[256,4096]{0,1:T(8,128)(2,1)} copy(bf16[256,4096]{1,0:T(8,128)(2,1)} %param.3) | data formatting | bytes 4194304 | tf_op args[0]
  4.3 3.9 %copy.13 = bf16[256,8,512]{2,0,1:T(8,128)(2,1)} copy(bf16[256,8,512]{0,2,1:T(8,128)(2,1)} %bitcast.75) | data formatting | bytes 4194304 | tf_op jit(solution)/shard_map/all_to_all | solution.py:328
  8.2 7.3 %all-to-all-start = ((bf16[256,8,512]{2,0,1:T(8,128)(2,1)}), bf16[256,8,512]{2,0,1:T(8,128)(2,1)}, u32[]{:S(2)}, u32[]{:S(2)}) async-start(bf16[256,8,512]{2,0,1:T(8,128)(2,1)} %copy.13), calls=%async_computation | async-start | bytes 4194304 | tf_op jit(solution)/shard_map/all_to_all | solution.py:328
  15.5 0.0 copy-done
  15.5 2.3 fusion.36.x_ref
  17.8 59.9 %start_sum.1 = bf16[8,256,256]{2,1,0:T(8,128)(2,1)S(1)} custom-call(f32[256,256]{1,0:T(8,128)S(1)} %fusion.36.x_ref), custom_call_target="tpu_custom_call" | custom-call | tf_op jit(solution)/shard_map/start_sum/pallas_call | solution.py:213
  78.4 0.0 all-to-all-done
  78.4 2.4 reduce-precision_convert_fusion.5
  80.8 3.4 %convolution_bitcast_fusion.2 = f32[2048,768]{1,0:T(8,128)S(1)} fusion(bf16[2048,512]{1,0:T(8,128)(2,1)} %bitcast.5, bf16[512,256]{0,1:T(8,128)(2,1)S(1)} %get-tuple-element.15, bf16[512,256]{0,1:T(8,128)(2,1)S(1)} %get-tuple-element.16, bf16[512,256]{0,1:T(8,128)(2,1)S(1)} %get-tuple-element.14), kind=kOutput, calls=%fused_computation.2 | convolution fusion | flops 1612972032 | bytes 9175040 | tf_op jit(solution)/shard_map/dot_general | solution.py:25
  84.2 0.4 fusion.2.x_ref
  84.6 44.5 %all_sum.3 = f32[2048,256]{1,0:T(8,128)S(1)} custom-call(f32[2048,256]{1,0:T(8,128)S(1)} %fusion.2.x_ref), custom_call_target="tpu_custom_call" | custom-call | tf_op jit(solution)/shard_map/all_sum/pallas_call | solution.py:121
  129.2 0.0 copy-start.1
  129.2 1.3 copy-done.1
  130.5 1.5 fusion.37
  132.0 0.1 copy.16
  132.1 0.7 fusion.29.gram_ref
  132.8 11.6 %factor.3 = f32[256,256]{1,0:T(8,128)} custom-call(f32[256,256]{1,0:T(8,128)} %fusion.29.gram_ref), custom_call_target="tpu_custom_call" | custom-call | tf_op jit(solution)/shard_map/factor/pallas_call | solution.py:314
  144.4 3.4 %convolution_convert_fusion.1 = bf16[2048,256]{1,0:T(8,128)(2,1)S(1)} fusion(f32[2048,256]{1,0:T(8,128)} %copy-done.1, f32[256,256]{1,0:T(8,128)} %factor.3), kind=kOutput, calls=%fused_computation.5 | convolution fusion | flops 1611137024 | bytes 3407872 | tf_op jit(solution)/shard_map/dot_general | solution.py:338
  147.9 2.4 reduce-precision_convert_fusion.3
  150.2 3.4 %convolution_bitcast_fusion.1 = f32[2048,768]{1,0:T(8,128)S(1)} fusion(bf16[2048,512]{1,0:T(8,128)(2,1)} %bitcast.5, bf16[512,256]{0,1:T(8,128)(2,1)S(1)} %get-tuple-element.12, bf16[512,256]{0,1:T(8,128)(2,1)S(1)} %get-tuple-element.13, bf16[512,256]{0,1:T(8,128)(2,1)S(1)} %get-tuple-element.11), kind=kOutput, calls=%fused_computation.1 | convolution fusion | flops 1612972032 | bytes 9175040 | tf_op jit(solution)/shard_map/dot_general | solution.py:25
  153.7 0.4 fusion.1.x_ref
  154.1 45.6 %all_sum.4 = f32[2048,256]{1,0:T(8,128)S(1)} custom-call(f32[2048,256]{1,0:T(8,128)S(1)} %fusion.1.x_ref), custom_call_target="tpu_custom_call" | custom-call | tf_op jit(solution)/shard_map/all_sum/pallas_call | solution.py:121
  199.6 0.0 copy-start.2
  199.7 1.3 copy-done.2
  200.9 1.5 fusion.38
  202.4 0.1 copy.18
  202.6 0.7 fusion.28.gram_ref
  203.3 11.6 %factor.4 = f32[256,256]{1,0:T(8,128)} custom-call(f32[256,256]{1,0:T(8,128)} %fusion.28.gram_ref), custom_call_target="tpu_custom_call" | custom-call | tf_op jit(solution)/shard_map/factor/pallas_call | solution.py:314
  214.9 3.4 %convolution_convert_fusion = bf16[2048,256]{1,0:T(8,128)(2,1)S(1)} fusion(f32[2048,256]{1,0:T(8,128)} %copy-done.2, f32[256,256]{1,0:T(8,128)} %factor.4), kind=kOutput, calls=%fused_computation.4 | convolution fusion | flops 1611137024 | bytes 3407872 | tf_op jit(solution)/shard_map/dot_general | solution.py:338
  218.4 2.4 reduce-precision_convert_fusion.1
  220.7 3.4 %convolution_bitcast_fusion = f32[2048,768]{1,0:T(8,128)S(1)} fusion(bf16[2048,512]{1,0:T(8,128)(2,1)} %bitcast.5, bf16[512,256]{0,1:T(8,128)(2,1)S(1)} %get-tuple-element.9, bf16[512,256]{0,1:T(8,128)(2,1)S(1)} %get-tuple-element.10, bf16[512,256]{0,1:T(8,128)(2,1)S(1)} %get-tuple-element.8), kind=kOutput, calls=%fused_computation | convolution fusion | flops 1612972032 | bytes 9175040 | tf_op jit(solution)/shard_map/dot_general | solution.py:25
  224.1 0.4 fusion.x_ref
  224.6 42.7 %all_sum.5 = f32[2048,256]{1,0:T(8,128)S(1)} custom-call(f32[2048,256]{1,0:T(8,128)S(1)} %fusion.x_ref), custom_call_target="tpu_custom_call" | custom-call | tf_op jit(solution)/shard_map/all_sum/pallas_call | solution.py:121
  267.3 0.0 copy-start.3
  267.3 1.3 copy-done.3
  268.6 1.5 fusion.39
  270.1 0.1 copy.20
  270.2 0.7 fusion.27.gram_ref
  271.0 11.7 %factor.5 = f32[256,256]{1,0:T(8,128)} custom-call(f32[256,256]{1,0:T(8,128)} %fusion.27.gram_ref), custom_call_target="tpu_custom_call" | custom-call | tf_op jit(solution)/shard_map/factor/pallas_call | solution.py:314
  282.6 3.5 %fusion.5 = f32[256]{0:T(256)S(1)} fusion(f32[2048,256]{1,0:T(8,128)} %copy-done.3, f32[256,256]{1,0:T(8,128)} %factor.5), kind=kOutput, calls=%fused_computation.14 | convolution fusion | flops 1611661056 | bytes 2360320 | tf_op jit(solution)/shard_map/dot_general | solution.py:338
  286.1 3.3 %sort.15 = (f32[256]{0:T(256)S(1)}, s32[256]{0:T(256)}) sort(f32[256]{0:T(256)S(1)} %fusion.5, s32[256]{0:T(256)S(1)} %iota.3), dimensions={0}, to_apply=%region_1.0 | sort | flops 2048 | bytes 4096 | tf_op jit(solution)/shard_map/jit(sort)/sort | solution.py:340
  289.4 0.1 rev.3
  289.5 0.6 dynamic_slice.4
  290.7 0.7 maximum_sqrt_fusion
  291.4 0.6 fusion.30
  292.1 20.1 %all_to_all.38 = f32[8,32,512]{2,1,0:T(8,128)S(1)} all-to-all(f32[8,32,512]{2,1,0:T(8,128)S(1)} %bitcast.76), channel_id=1, replica_groups=mesh['rows'=8,'cols'=4] {'rows'}, dimensions={0} | all-to-all | bytes 1048576 | tf_op jit(solution)/shard_map/all_to_all | solution.py:344
  312.1 0.8 copy.26
  (3 shorter events, 0.0 us)
Async XLA Ops:
  0.0 15.5 %copy-start = (bf16[4096,256]{1,0:T(8,128)(2,1)S(1)}, bf16[4096,256]{1,0:T(8,128)(2,1)}, u32[]{:S(2)}) copy-start(bf16[4096,256]{1,0:T(8,128)(2,1)} %param.4) | copy-start | bytes 6291460
  8.2 70.2 %all-to-all-start = ((bf16[256,8,512]{2,0,1:T(8,128)(2,1)}), bf16[256,8,512]{2,0,1:T(8,128)(2,1)}, u32[]{:S(2)}, u32[]{:S(2)}) async-start(bf16[256,8,512]{2,0,1:T(8,128)(2,1)} %copy.13), calls=%async_computation | async-start | bytes 4194304 | tf_op jit(solution)/shard_map/all_to_all | solution.py:328
  129.2 1.3 copy-start.1
  199.6 1.3 copy-start.2
  267.3 1.4 copy-start.3
  282.6 8.8 %copy-start.4 = (f32[256,256]{1,0:T(8,128)S(1)}, f32[256,256]{1,0:T(8,128)}, u32[]{:S(2)}) copy-start(f32[256,256]{1,0:T(8,128)} %factor.5) | copy-start | bytes 786436
where the time goes:
time: 314 us; the launch traced here: 313 us
  Pallas kernels  228 us (73%)
  matrix products  35 us (11%)
  blocking collectives  20.1 us (6%)
  local copies, waits for them, and re-layouts  14 us (4%)
  other arithmetic  7.34 us (2%)
  starting transfers between devices  7.31 us (2%)
    pallas_call x3, Pallas kernels, all_sum(): pl.pallas_call(functools.partial(sum_kernel, orders), out_shape=jax.Shape...  133 us
    pallas_call x1, Pallas kernels, start_sum(): pl.pallas_call(functools.partial(start_kernel, sizes), out_shape=jax.Shap...  59.9 us
    pallas_call x3, Pallas kernels, inverse_factor(): pl.pallas_call(factor_kernel, out_shape=jax.ShapeDtypeStruct(gram_total.s...  34.9 us
    all_to_all x1, blocking collectives, body(): lax.all_to_all(scaled, 'rows', split_axis=0, concat_axis=1, tiled=True)  20.1 us
    dot_general x3, matrix products, body(): projected = jnp.dot(raw, inverse.T, precision=HIGHEST)  10.3 us
    dot_general x3, matrix products, apply_sketches(): products = jnp.dot(strip, stacked, preferred_element_type=jnp.float32)  10.2 us
    unnamed x11, local copies, waits for them, and re-layouts  8.18 us
    all_to_all x1, starting transfers between devices, body(): lax.all_to_all(sketches, 'rows', split_axis=1, concat_axis=0, tiled=True)  7.31 us
  transfers between devices with their start and end apart: 1, of which 0 were waited for; matrix products, arithmetic and copies ran while one was open for 1% of the time, Pallas kernels for 19%

commit v1 on v0

--- a/solution.py
+++ b/solution.py
@@ -31,8 +31,8 @@
     cols_bits = [("cols", 1 << bit) for bit in range(sizes["cols"].bit_length() - 1)]
     rows_bits = [("rows", 1 << bit) for bit in range(sizes["rows"].bit_length() - 1)]
     first = cols_bits + rows_bits
-    second = cols_bits[:1] + rows_bits + cols_bits[1:]
-    return [first, second]
+    second = cols_bits[:1] + rows_bits[:1] + cols_bits[1:] + rows_bits[1:]
+    return [first, second] * 2
 
 
 def sum_kernel(orders, x_ref, out_ref, partial, arrived, send_sems, recv_sems):

time: 314 us -> 293 us (0.933)
  Pallas kernels: 228 us -> 208 us
    pallas_call x3, Pallas kernels: 133 us -> 113 us  [all_sum(): pl.pallas_call(functools.partial(sum_kernel, orders), out_shape=jax.Shape...]
  transfers between devices with their start and end apart: 1 -> 1, of which waited for: 0 -> 0; matrix products, arithmetic and copies ran while one was open for 1% -> 1% of each run, Pallas kernels for 19% -> 21%
where the time goes in v1:
time: 293 us; the launch traced here: 292 us
  Pallas kernels  208 us (71%)
  matrix products  35 us (12%)
  blocking collectives  19.1 us (7%)
  local copies, waits for them, and re-layouts  14 us (5%)
  other arithmetic  7.34 us (3%)
  starting transfers between devices  7.31 us (2%)
    pallas_call x3, Pallas kernels, all_sum(): pl.pallas_call(functools.partial(sum_kernel, orders), out_shape=jax.Shape...  113 us
    pallas_call x1, Pallas kernels, start_sum(): pl.pallas_call(functools.partial(start_kernel, sizes), out_shape=jax.Shap...  59.9 us
    pallas_call x3, Pallas kernels, inverse_factor(): pl.pallas_call(factor_kernel, out_shape=jax.ShapeDtypeStruct(gram_total.s...  34.9 us
    all_to_all x1, blocking collectives, body(): lax.all_to_all(scaled, 'rows', split_axis=0, concat_axis=1, tiled=True)  19.1 us
    dot_general x3, matrix products, body(): projected = jnp.dot(raw, inverse.T, precision=HIGHEST)  10.3 us
    dot_general x3, matrix products, apply_sketches(): products = jnp.dot(strip, stacked, preferred_element_type=jnp.float32)  10.2 us
    unnamed x11, local copies, waits for them, and re-layouts  8.18 us
    all_to_all x1, starting transfers between devices, body(): lax.all_to_all(sketches, 'rows', split_axis=1, concat_axis=0, tiled=True)  7.31 us
  transfers between devices with their start and end apart: 1, of which 0 were waited for; matrix products, arithmetic and copies ran while one was open for 1% of the time, Pallas kernels for 21%

profile of v1, /device:TPU:0, one launch (start us, length us, event | category | flops | bytes accessed | tf_op | source)
XLA Modules:
  0.0 292.3 jit_solution(5970698335380617865)
XLA Ops:
  0.0 0.0 copy-start
  0.0 4.3 %copy.12 = bf16[256,4096]{0,1:T(8,128)(2,1)} copy(bf16[256,4096]{1,0:T(8,128)(2,1)} %param.3) | data formatting | bytes 4194304 | tf_op args[0]
  4.3 3.9 %copy.13 = bf16[256,8,512]{2,0,1:T(8,128)(2,1)} copy(bf16[256,8,512]{0,2,1:T(8,128)(2,1)} %bitcast.75) | data formatting | bytes 4194304 | tf_op jit(solution)/shard_map/all_to_all | solution.py:328
  8.2 7.3 %all-to-all-start = ((bf16[256,8,512]{2,0,1:T(8,128)(2,1)}), bf16[256,8,512]{2,0,1:T(8,128)(2,1)}, u32[]{:S(2)}, u32[]{:S(2)}) async-start(bf16[256,8,512]{2,0,1:T(8,128)(2,1)} %copy.13), calls=%async_computation | async-start | bytes 4194304 | tf_op jit(solution)/shard_map/all_to_all | solution.py:328
  15.5 0.0 copy-done
  15.5 2.3 fusion.36.x_ref
  17.8 59.9 %start_sum.1 = bf16[8,256,256]{2,1,0:T(8,128)(2,1)S(1)} custom-call(f32[256,256]{1,0:T(8,128)S(1)} %fusion.36.x_ref), custom_call_target="tpu_custom_call" | custom-call | tf_op jit(solution)/shard_map/start_sum/pallas_call | solution.py:213
  78.4 0.0 all-to-all-done
  78.4 2.4 reduce-precision_convert_fusion.5
  80.8 3.4 %convolution_bitcast_fusion.2 = f32[2048,768]{1,0:T(8,128)S(1)} fusion(bf16[2048,512]{1,0:T(8,128)(2,1)} %bitcast.5, bf16[512,256]{0,1:T(8,128)(2,1)S(1)} %get-tuple-element.15, bf16[512,256]{0,1:T(8,128)(2,1)S(1)} %get-tuple-element.16, bf16[512,256]{0,1:T(8,128)(2,1)S(1)} %get-tuple-element.14), kind=kOutput, calls=%fused_computation.2 | convolution fusion | flops 1612972032 | bytes 9175040 | tf_op jit(solution)/shard_map/dot_general | solution.py:25
  84.2 0.4 fusion.2.x_ref
  84.6 37.6 %all_sum.3 = f32[2048,256]{1,0:T(8,128)S(1)} custom-call(f32[2048,256]{1,0:T(8,128)S(1)} %fusion.2.x_ref), custom_call_target="tpu_custom_call" | custom-call | tf_op jit(solution)/shard_map/all_sum/pallas_call | solution.py:121
  122.2 0.0 copy-start.1
  122.2 1.3 copy-done.1
  123.5 1.5 fusion.37
  125.0 0.1 copy.16
  125.1 0.7 fusion.29.gram_ref
  125.9 11.6 %factor.3 = f32[256,256]{1,0:T(8,128)} custom-call(f32[256,256]{1,0:T(8,128)} %fusion.29.gram_ref), custom_call_target="tpu_custom_call" | custom-call | tf_op jit(solution)/shard_map/factor/pallas_call | solution.py:314
  137.5 3.4 %convolution_convert_fusion.1 = bf16[2048,256]{1,0:T(8,128)(2,1)S(1)} fusion(f32[2048,256]{1,0:T(8,128)} %copy-done.1, f32[256,256]{1,0:T(8,128)} %factor.3), kind=kOutput, calls=%fused_computation.5 | convolution fusion | flops 1611137024 | bytes 3407872 | tf_op jit(solution)/shard_map/dot_general | solution.py:338
  140.9 2.4 reduce-precision_convert_fusion.3
  143.3 3.4 %convolution_bitcast_fusion.1 = f32[2048,768]{1,0:T(8,128)S(1)} fusion(bf16[2048,512]{1,0:T(8,128)(2,1)} %bitcast.5, bf16[512,256]{0,1:T(8,128)(2,1)S(1)} %get-tuple-element.12, bf16[512,256]{0,1:T(8,128)(2,1)S(1)} %get-tuple-element.13, bf16[512,256]{0,1:T(8,128)(2,1)S(1)} %get-tuple-element.11), kind=kOutput, calls=%fused_computation.1 | convolution fusion | flops 1612972032 | bytes 9175040 | tf_op jit(solution)/shard_map/dot_general | solution.py:25
  146.7 0.4 fusion.1.x_ref
  147.1 38.7 %all_sum.4 = f32[2048,256]{1,0:T(8,128)S(1)} custom-call(f32[2048,256]{1,0:T(8,128)S(1)} %fusion.1.x_ref), custom_call_target="tpu_custom_call" | custom-call | tf_op jit(solution)/shard_map/all_sum/pallas_call | solution.py:121
  185.8 0.0 copy-start.2
  185.8 1.3 copy-done.2
  187.1 1.5 fusion.38
  188.6 0.1 copy.18
  188.8 0.7 fusion.28.gram_ref
  189.5 11.6 %factor.4 = f32[256,256]{1,0:T(8,128)} custom-call(f32[256,256]{1,0:T(8,128)} %fusion.28.gram_ref), custom_call_target="tpu_custom_call" | custom-call | tf_op jit(solution)/shard_map/factor/pallas_call | solution.py:314
  201.1 3.4 %convolution_convert_fusion = bf16[2048,256]{1,0:T(8,128)(2,1)S(1)} fusion(f32[2048,256]{1,0:T(8,128)} %copy-done.2, f32[256,256]{1,0:T(8,128)} %factor.4), kind=kOutput, calls=%fused_computation.4 | convolution fusion | flops 1611137024 | bytes 3407872 | tf_op jit(solution)/shard_map/dot_general | solution.py:338
  204.6 2.4 reduce-precision_convert_fusion.1
  206.9 3.4 %convolution_bitcast_fusion = f32[2048,768]{1,0:T(8,128)S(1)} fusion(bf16[2048,512]{1,0:T(8,128)(2,1)} %bitcast.5, bf16[512,256]{0,1:T(8,128)(2,1)S(1)} %get-tuple-element.9, bf16[512,256]{0,1:T(8,128)(2,1)S(1)} %get-tuple-element.10, bf16[512,256]{0,1:T(8,128)(2,1)S(1)} %get-tuple-element.8), kind=kOutput, calls=%fused_computation | convolution fusion | flops 1612972032 | bytes 9175040 | tf_op jit(solution)/shard_map/dot_general | solution.py:25
  210.3 0.4 fusion.x_ref
  210.8 36.9 %all_sum.5 = f32[2048,256]{1,0:T(8,128)S(1)} custom-call(f32[2048,256]{1,0:T(8,128)S(1)} %fusion.x_ref), custom_call_target="tpu_custom_call" | custom-call | tf_op jit(solution)/shard_map/all_sum/pallas_call | solution.py:121
  247.6 1.3 copy-done.3
  249.0 1.5 fusion.39
  250.5 0.1 copy.20
  250.6 0.7 fusion.27.gram_ref
  251.4 11.7 %factor.5 = f32[256,256]{1,0:T(8,128)} custom-call(f32[256,256]{1,0:T(8,128)} %fusion.27.gram_ref), custom_call_target="tpu_custom_call" | custom-call | tf_op jit(solution)/shard_map/factor/pallas_call | solution.py:314
  263.0 3.5 %fusion.5 = f32[256]{0:T(256)S(1)} fusion(f32[2048,256]{1,0:T(8,128)} %copy-done.3, f32[256,256]{1,0:T(8,128)} %factor.5), kind=kOutput, calls=%fused_computation.14 | convolution fusion | flops 1611661056 | bytes 2360320 | tf_op jit(solution)/shard_map/dot_general | solution.py:338
  266.5 3.3 %sort.15 = (f32[256]{0:T(256)S(1)}, s32[256]{0:T(256)}) sort(f32[256]{0:T(256)S(1)} %fusion.5, s32[256]{0:T(256)S(1)} %iota.3), dimensions={0}, to_apply=%region_1.0 | sort | flops 2048 | bytes 4096 | tf_op jit(solution)/shard_map/jit(sort)/sort | solution.py:340
  269.8 0.1 rev.3
  269.9 0.6 dynamic_slice.4
  271.1 0.7 maximum_sqrt_fusion
  271.8 0.0 copy-done.4
  271.8 0.6 fusion.30
  272.4 19.1 %all_to_all.38 = f32[8,32,512]{2,1,0:T(8,128)S(1)} all-to-all(f32[8,32,512]{2,1,0:T(8,128)S(1)} %bitcast.76), channel_id=1, replica_groups=mesh['rows'=8,'cols'=4] {'rows'}, dimensions={0} | all-to-all | bytes 1048576 | tf_op jit(solution)/shard_map/all_to_all | solution.py:344
  291.5 0.8 copy.26
  (3 shorter events, 0.0 us)
Async XLA Ops:
  0.0 15.5 %copy-start = (bf16[4096,256]{1,0:T(8,128)(2,1)S(1)}, bf16[4096,256]{1,0:T(8,128)(2,1)}, u32[]{:S(2)}) copy-start(bf16[4096,256]{1,0:T(8,128)(2,1)} %param.4) | copy-start | bytes 6291460
  8.2 70.2 %all-to-all-start = ((bf16[256,8,512]{2,0,1:T(8,128)(2,1)}), bf16[256,8,512]{2,0,1:T(8,128)(2,1)}, u32[]{:S(2)}, u32[]{:S(2)}) async-start(bf16[256,8,512]{2,0,1:T(8,128)(2,1)} %copy.13), calls=%async_computation | async-start | bytes 4194304 | tf_op jit(solution)/shard_map/all_to_all | solution.py:328
  122.2 1.3 copy-start.1
  185.8 1.3 copy-start.2
  247.6 1.4 copy-start.3
  263.0 8.8 %copy-start.4 = (f32[256,256]{1,0:T(8,128)S(1)}, f32[256,256]{1,0:T(8,128)}, u32[]{:S(2)}) copy-start(f32[256,256]{1,0:T(8,128)} %factor.5) | copy-start | bytes 786436
